TPU v7x, 32 devices: a whole 2x2x4 slice. The times are simulated.
32 devices in a mesh: groups: 2 (over y), mom: 4 (over z), tm: 2 (over x), spin: 2 (over core).
Axes of the slice: x: 2, y: 2, z: 4, core: 2. Of those that a mesh axis runs over, the one named last changes fastest.
Arguments:
- fields: bfloat16 [32, 2, 2, 2, 256, 256], P(('groups', 'mom'), 'tm', 'spin'), parts along dimension 0, may hold values from -1.5 to 1.5
- pair_slot: int32 [2, 4, 4, 3], replicated, may hold values from 0 to 3, as said below
- channel: int32 [2, 4, 4, 3], replicated, may hold values from 0 to 3
- cg_index: int32 [2, 4, 4, 3], replicated, may hold values from 0 to 63
- cg_table: float32 [64], replicated, may hold values from -0.6 to 0.6
Outputs:
- operators: bfloat16 [4, 4, 2, 2, 256, 256], P(None, ('groups', 'tm'), 'spin', None, 'mom'), parts along dimension 1
There are 2 independent parts, one for each index of `groups`. A program takes and returns all parts, laid end to end along the dimension named above; an argument that names none is the same for every part. Nothing has to cross between parts.
Inputs may be any that keep to these rules, and one draw needn't show every extreme that they name: For every round and every index of mom, the 4 x 3 entries of pair_slot take exactly 2 distinct values.
All inputs are finite; a program needn't handle non-finite values.
Results may differ from a plain program's by a relative error of at most 0.0012.
Values may be sent and summed in bfloat16 or wider, within the bound.
No kernel may reach another device: no remote copies, remote signals or barrier semaphores. Data moves between devices by JAX's collectives and lax.ppermute only.
A program may use at most 64 MiB of HBM per device.

v0:
```python
import jax
import jax.numpy as jnp
from jax import lax
from jax.sharding import PartitionSpec as P

ROUNDS = 2
CHANNELS = 4


def from_partner(block, axis, stride):
    count = lax.axis_size(axis)
    route = []
    for low in range(count):
        high = low | 1 << stride
        if high != low and high < count:
            route += [(low, high), (high, low)]
    return lax.ppermute(block, axis, route)


def complex_single(left_block, right_block):
    form = "tgxy,tgyz->tgxz"
    left_real = left_block[:, :, 0]
    left_imag = left_block[:, :, 1]
    right_real = right_block[:, :, 0]
    right_imag = right_block[:, :, 1]
    real_part = jnp.einsum(
        form, left_real, right_real, preferred_element_type=jnp.float32
    ) - jnp.einsum(form, left_imag, right_imag, preferred_element_type=jnp.float32)
    imag_part = jnp.einsum(
        form, left_real, right_imag, preferred_element_type=jnp.float32
    ) + jnp.einsum(form, left_imag, right_real, preferred_element_type=jnp.float32)
    return jnp.stack([real_part, imag_part], axis=2)


def per_device(fields, pair_slot, channel, cg_index, cg_table):
    mom_dev = fields.shape[0]
    pair_count = pair_slot.shape[3]
    axis_size = lax.axis_size("mom")
    log_size = axis_size.bit_length() - 1
    device_idx = lax.axis_index("mom")
    accumulated = jnp.zeros((CHANNELS,) + fields.shape[1:], jnp.float32)
    for round_idx in range(ROUNDS):
        shift_bit = (log_size - 1 - round_idx) % log_size
        own_row = pair_slot[round_idx][device_idx]
        remote = from_partner(fields, "mom", shift_bit)
        chan_rows = channel[round_idx][device_idx]
        index_rows = cg_index[round_idx][device_idx]
        for slot_idx in range(mom_dev):
            left_block = fields[slot_idx]
            for pair_idx in range(pair_count):
                right_block = lax.dynamic_index_in_dim(
                    remote, own_row[slot_idx, pair_idx], 0, keepdims=False
                )
                weight = lax.dynamic_index_in_dim(
                    cg_table, index_rows[slot_idx, pair_idx], 0, keepdims=False
                )
                target = chan_rows[slot_idx, pair_idx]
                term = weight * complex_single(left_block, right_block)
                current = lax.dynamic_index_in_dim(accumulated, target, 0, keepdims=False)
                accumulated = lax.dynamic_update_index_in_dim(
                    accumulated, current + term, target, 0
                )
    summed = lax.psum_scatter(accumulated, "mom", scatter_dimension=4, tiled=True)
    return summed.astype(jnp.bfloat16)


def solution(mesh):
    placed = (P(("groups", "mom"), "tm", "spin", None, None, None), P(), P(), P(), P())
    return jax.shard_map(
        per_device,
        mesh=mesh,
        in_specs=placed,
        out_specs=P(None, ("groups", "tm"), "spin", None, "mom", None),
        check_vma=False,
    )
```

profile of v0, /device:TPU:0, one launch (start us, length us, event | category | flops | bytes accessed | tf_op | source)
XLA Modules:
  0.0 271.7 jit_solution(91739074095331115)
XLA Ops:
  0.0 4.1 %collective-permute-start = (bf16[4,1,1,2,256,256]{5,4,3,2,1,0:T(8,128)(2,1)}, bf16[4,1,1,2,256,256]{5,4,3,2,1,0:T(8,128)(2,1)S(1)}, u32[]{:S(2)}, u32[]{:S(2)}) collective-permute-start(bf16[4,1,1,2,256,256]{5,4,3,2,1,0:T(8,128)(2,1)} %param.5), channel_id=1, source_target_pairs={{0,8},{8,0},{4,12},{12,4},{1,9},{9,1},{5,13},{13,5},{2,10},{10,2},... | collective-permute-start | bytes 3145736 | tf_op jit(solution)/shard_map/ppermute | solution.py:17
  4.1 1.6 collective-permute-start.1
  5.6 0.7 fusion.145
  6.4 0.7 fusion.144
  7.2 0.7 fusion.151
  9.3 0.7 fusion.143
  10.0 0.7 fusion.150
  147.4 1.2 dynamic-slice.6
  149.3 1.6 fusion.153
  150.9 2.0 fusion.152
  152.9 1.3 slice_bitcast_fusion
  177.7 0.8 fusion.50
  178.5 0.8 fusion.52
  179.9 0.7 fusion.56
  181.3 0.8 fusion.60
  182.1 0.8 fusion.62
  183.6 0.7 fusion.66
  184.3 0.7 fusion.68
  185.7 0.8 fusion.72
  186.5 0.7 fusion.74
  187.2 0.7 fusion.76
  188.0 0.8 fusion.78
  188.8 0.8 fusion.80
  190.2 0.8 fusion.84
  191.0 0.7 fusion.86
  191.7 0.7 fusion.88
  192.5 0.7 fusion.90
  193.2 0.7 fusion.92
  194.0 0.7 fusion.94
  194.7 2.0 copy.19
  196.7 74.1 %all-reduce.2 = bf16[4,1,1,2,256,256]{5,0,3,2,1,4:T(4,128)(2,1)S(1)} all-reduce(f32[4,1,1,2,256,256]{5,0,3,2,1,4:T(4,128)} %copy.19), channel_id=2, replica_groups=mesh['groups'=2,'mom'=4,'tm'=2,'spin'=2] {'mom'}, use_global_device_ids=true, to_apply=%region_0.1.clone | all-reduce | flops 524288 | bytes 3145728
  270.9 0.8 copy.20
  (121 shorter events, 29.5 us)
Async XLA Ops:
  0.0 154.2 %collective-permute-start = (bf16[4,1,1,2,256,256]{5,4,3,2,1,0:T(8,128)(2,1)}, bf16[4,1,1,2,256,256]{5,4,3,2,1,0:T(8,128)(2,1)S(1)}, u32[]{:S(2)}, u32[]{:S(2)}) collective-permute-start(bf16[4,1,1,2,256,256]{5,4,3,2,1,0:T(8,128)(2,1)} %param.5), channel_id=1, source_target_pairs={{0,8},{8,0},{4,12},{12,4},{1,9},{9,1},{5,13},{13,5},{2,10},{10,2},... | collective-permute-start | bytes 3145736 | tf_op jit(solution)/shard_map/ppermute | solution.py:17
  4.1 155.8 %collective-permute-start.1 = (bf16[4,1,1,2,256,256]{5,4,3,2,1,0:T(8,128)(2,1)}, bf16[4,1,1,2,256,256]{5,4,3,2,1,0:T(8,128)(2,1)S(1)}, u32[]{:S(2)}, u32[]{:S(2)}) collective-permute-start(bf16[4,1,1,2,256,256]{5,4,3,2,1,0:T(8,128)(2,1)} %param.5), channel_id=1, source_target_pairs={{0,4},{4,0},{8,12},{12,8},{1,5},{5,1},{9,13},{13,9},{2,6},{6,2},{1... | collective-permute-start | bytes 3145736 | tf_op jit(solution)/shard_map/ppermute | solution.py:17
where the time goes:
time: 274 us; the launch traced here: 272 us
  between operations  136 us (50%)
  blocking collectives  74.1 us (27%)
  matrix products  21.5 us (8%)
  other arithmetic  17.5 us (6%)
  local copies, waits for them, and re-layouts  16.5 us (6%)
  starting transfers between devices  5.64 us (2%)
    unnamed x1, blocking collectives  74.1 us
    dynamic_update_slice x24, other arithmetic, per_device(): lax.dynamic_update_index_in_dim(accumulated, current + term, target, 0)  17.5 us
    ppermute x2, starting transfers between devices, from_partner(): return lax.ppermute(block, axis, route)  5.64 us
  transfers between devices with their start and end apart: 2, of which 0 were waited for; matrix products, arithmetic and copies ran while one was open for 7% of the time, Pallas kernels for 0%

commit v1 on v0

v1 whole, which is shorter than its diff:
```python
import functools

import jax
import jax.numpy as jnp
from jax import lax
from jax.experimental import pallas as pl
from jax.experimental.pallas import tpu as pltpu
from jax.sharding import PartitionSpec as P

ROUNDS = 2
CHANNELS = 4
SLOTS = 2
CHUNKS = 2
LEVELS = 32000.0
SCALE_ROWS = 16
LOWEST, HIGHEST = -110, 31

VMEM = pl.BlockSpec(memory_space=pltpu.VMEM)
SMEM = pl.BlockSpec(memory_space=pltpu.SMEM)


def two_slots(pair_slot, round_idx, index, mom_dev, pair_count):
    entries = [pair_slot[round_idx, index, s, k] for s in range(mom_dev) for k in range(pair_count)]
    return functools.reduce(jnp.minimum, entries), functools.reduce(jnp.maximum, entries)


def exact_power(exponent):
    size = jnp.abs(exponent)
    negative = exponent < 0
    power = jnp.ones(exponent.shape, jnp.float32)
    for bit in range(7):
        step = jnp.where(negative, 2.0 ** -(1 << bit), 2.0 ** (1 << bit))
        power = jnp.where((size >> bit) & 1 == 1, power * step, power)
    return power


def pick_kernel(bits, pair_slot, fields, *outs):
    mom_dev, pair_count = pair_slot.shape[2], pair_slot.shape[3]
    me = lax.axis_index("mom")
    width = outs[0].shape[-1]
    for r, bit in enumerate(bits):
        slots = two_slots(pair_slot, r, me ^ bit, mom_dev, pair_count)
        for d, slot in enumerate(slots):
            block = fields[slot]
            for q in range(CHUNKS):
                outs[q * ROUNDS + r][d] = block[:, :, q * width : (q + 1) * width]


def product_kernel(count, pair_slot, channel, cg_index, cg_table, fields, *refs):
    rights, (own, *sent), (weights, packed) = refs[:ROUNDS], refs[ROUNDS : ROUNDS + count], refs[ROUNDS + count :]
    mom_dev, pair_count = pair_slot.shape[2], pair_slot.shape[3]
    modes, width = fields.shape[2], rights[0].shape[-1]
    rows = modes // count
    me = lax.axis_index("mom")

    for i in range(ROUNDS * SLOTS * mom_dev * CHANNELS):
        weights[i] = jnp.float32(0)
    for r in range(ROUNDS):
        low, _ = two_slots(pair_slot, r, me, mom_dev, pair_count)
        for s in range(mom_dev):
            for k in range(pair_count):
                d = jnp.where(pair_slot[r, me, s, k] == low, 0, 1)
                at = ((r * SLOTS + d) * mom_dev + s) * CHANNELS + channel[r, me, s, k]
                weights[at] = weights[at] + cg_table[cg_index[r, me, s, k]]

    for r in range(ROUNDS):
        for d in range(SLOTS):
            real, imag = rights[r][d, 0], rights[r][d, 1]
            packed[r * SLOTS + d, :modes, :width] = real
            packed[r * SLOTS + d, :modes, width:] = imag
            packed[r * SLOTS + d, modes:, :width] = -imag
            packed[r * SLOTS + d, modes:, width:] = real

    for hop in [*range(1, count), 0]:
        start = pl.multiple_of((me ^ hop) * rows, rows)
        left = jnp.concatenate(
            [
                jnp.concatenate([fields[s, 0, pl.ds(start, rows), :], fields[s, 1, pl.ds(start, rows), :]], axis=1)
                for s in range(mom_dev)
            ],
            axis=0,
        )
        totals = [None] * CHANNELS
        for rd in range(ROUNDS * SLOTS):
            term = jnp.dot(left, packed[rd], preferred_element_type=jnp.float32)
            for s in range(mom_dev):
                part = term[s * rows : (s + 1) * rows]
                for c in range(CHANNELS):
                    weighted = weights[(rd * mom_dev + s) * CHANNELS + c] * part
                    totals[c] = weighted if totals[c] is None else totals[c] + weighted
        if hop == 0:
            for c in range(CHANNELS):
                own[(2 * c) * rows : (2 * c + 1) * rows] = totals[c][:, :width]
                own[(2 * c + 1) * rows : (2 * c + 2) * rows] = totals[c][:, width:]
        else:
            out = sent[hop - 1]
            row_id = lax.broadcasted_iota(jnp.int32, (SCALE_ROWS, width), 0)
            kept = jnp.zeros((SCALE_ROWS, width), jnp.int32)
            for c in range(CHANNELS):
                most = jnp.max(jnp.abs(totals[c]), axis=0, keepdims=True)
                exponent = jnp.ceil(jnp.log2(jnp.maximum(most, 2.0**LOWEST))).astype(jnp.int32)
                exponent = jnp.minimum(jnp.maximum(exponent, LOWEST), HIGHEST)
                coded = jnp.round(totals[c] * (exact_power(-exponent) * LEVELS)).astype(jnp.int32)
                for p in range(2):
                    at = 2 * c + p
                    out[at * rows : (at + 1) * rows] = coded[:, p * width : (p + 1) * width].astype(jnp.int16)
                    kept = jnp.where(row_id == at, exponent[:, p * width : (p + 1) * width], kept)
            out[2 * CHANNELS * rows :] = kept.astype(jnp.int16)


def total_kernel(count, *refs):
    ins, out = refs[:-1], refs[-1]
    rows, width = out.shape[2], ins[0].shape[-1]
    for q in range(CHUNKS):
        own, *came = ins[q * count : (q + 1) * count]
        for hop in came:
            assert hop.shape[1] == width
        scales = [
            exact_power(hop[2 * CHANNELS * rows :].astype(jnp.int32)) * (1.0 / LEVELS) for hop in came
        ]
        for at in range(2 * CHANNELS):
            total = own[at * rows : (at + 1) * rows]
            for hop, scale in zip(came, scales):
                total = total + hop[at * rows : (at + 1) * rows].astype(jnp.float32) * scale[at : at + 1]
            out[at // 2, at % 2, :, q * width : (q + 1) * width] = total.astype(out.dtype)


def per_device(fields, pair_slot, channel, cg_index, cg_table):
    mom_dev, modes = fields.shape[0], fields.shape[-1]
    count = lax.axis_size("mom")
    log_size = count.bit_length() - 1
    bits = [1 << ((log_size - 1 - r) % log_size) for r in range(ROUNDS)]
    rows, width = modes // count, modes // CHUNKS
    blocks = fields.reshape(mom_dev, 2, modes, modes)

    def exchange(x, bit):
        return lax.ppermute(x, "mom", [(i, i ^ bit) for i in range(count)])

    picked = pl.pallas_call(
        functools.partial(pick_kernel, bits),
        out_shape=[jax.ShapeDtypeStruct((SLOTS, 2, modes, width), fields.dtype)] * (CHUNKS * ROUNDS),
        in_specs=[SMEM, VMEM],
        out_specs=[VMEM] * (CHUNKS * ROUNDS),
        name="pick",
    )(pair_slot, blocks)
    rights = [exchange(picked[q * ROUNDS + r], bits[r]) for q in range(CHUNKS) for r in range(ROUNDS)]

    flat = 2 * CHANNELS * rows
    products = pl.pallas_call(
        functools.partial(product_kernel, count),
        out_shape=[jax.ShapeDtypeStruct((flat, width), jnp.float32)]
        + [jax.ShapeDtypeStruct((flat + SCALE_ROWS, width), jnp.int16)] * (count - 1),
        in_specs=[SMEM] * 4 + [VMEM] * (1 + ROUNDS),
        out_specs=[VMEM] * count,
        scratch_shapes=[
            pltpu.SMEM((ROUNDS * SLOTS * mom_dev * CHANNELS,), jnp.float32),
            pltpu.VMEM((ROUNDS * SLOTS, 2 * modes, 2 * width), fields.dtype),
        ],
        cost_estimate=pl.CostEstimate(
            flops=ROUNDS * SLOTS * mom_dev * 8 * modes * modes * width,
            bytes_accessed=4 * modes * modes * mom_dev,
            transcendentals=0,
        ),
        name="products",
    )
    gathered = []
    for q in range(CHUNKS):
        own, *sent = products(
            pair_slot, channel, cg_index, cg_table, blocks, *rights[q * ROUNDS : (q + 1) * ROUNDS]
        )
        gathered += [own] + [exchange(block, hop + 1) for hop, block in enumerate(sent)]

    out = pl.pallas_call(
        functools.partial(total_kernel, count),
        out_shape=jax.ShapeDtypeStruct((CHANNELS, 2, rows, modes), jnp.bfloat16),
        in_specs=[VMEM] * len(gathered),
        out_specs=VMEM,
        name="total",
    )(*gathered)
    return out.reshape(CHANNELS, 1, 1, 2, rows, modes)


def solution(mesh):
    placed = (P(("groups", "mom"), "tm", "spin", None, None, None), P(), P(), P(), P())
    return jax.shard_map(
        per_device,
        mesh=mesh,
        in_specs=placed,
        out_specs=P(None, ("groups", "tm"), "spin", None, "mom", None),
        check_vma=False,
    )
```

time: 274 us -> 56.8 us (0.21)
  between operations: 136 us -> 0.07 us
  blocking collectives: 74.1 us -> 0 us
  waiting for transfers between devices: 0.01 us -> 21.9 us
  matrix products: 21.5 us -> 0 us
  other arithmetic: 17.5 us -> 0 us
  Pallas kernels: 0 us -> 14.1 us
  local copies, waits for them, and re-layouts: 16.5 us -> 5.65 us
  starting transfers between devices: 5.64 us -> 14.9 us
    unnamed x1 -> x0, blocking collectives: 74.1 us -> none
    ppermute x2 -> x10, waiting for transfers between devices: 0.01 us -> 21.9 us  [exchange(): return lax.ppermute(x, 'mom', [(i, i ^ bit) for i in range(count)])]
    dot_general x96 -> x0, matrix products: 21.5 us -> none  [the longest x24 5.44 us: complex_single(): jnp.einsum(form, left_real, right_real, preferred_element_type=jnp.float32)]
    dynamic_update_slice x24 -> x0, other arithmetic: 17.5 us -> none  [per_device(): lax.dynamic_update_index_in_dim(accumulated, current + term, target, 0)]
    pallas_call x0 -> x4, Pallas kernels: none -> 14.1 us  [the longest x2 9.38 us: per_device(): products(pair_slot, channel, cg_index, cg_table, blocks, *rights[q * ROUN...]
    ppermute x2 -> x10, starting transfers between devices: 5.64 us -> 14.9 us  [exchange(): return lax.ppermute(x, 'mom', [(i, i ^ bit) for i in range(count)])]
    slice x9 -> x0, local copies, waits for them, and re-layouts: 6.28 us -> none  [the longest x2 1.39 us: per_device(): own_row[slot_idx, pair_idx]]
    unnamed x1 -> x27, local copies, waits for them, and re-layouts: 1.24 us -> 5.65 us
  transfers between devices with their start and end apart: 2 -> 10, of which waited for: 0 -> 4; matrix products, arithmetic and copies ran while one was open for 7% -> 3% of each run, Pallas kernels for 0% -> 17%
where the time goes in v1:
time: 56.8 us; the launch traced here: 56.5 us
  waiting for transfers between devices  21.9 us (39%)
  starting transfers between devices  14.9 us (26%)
  Pallas kernels  14.1 us (25%)
  local copies, waits for them, and re-layouts  5.65 us (10%)
    ppermute x10, waiting for transfers between devices, exchange(): return lax.ppermute(x, 'mom', [(i, i ^ bit) for i in range(count)])  21.9 us
    ppermute x10, starting transfers between devices, exchange(): return lax.ppermute(x, 'mom', [(i, i ^ bit) for i in range(count)])  14.9 us
    pallas_call x2, Pallas kernels, per_device(): products(pair_slot, channel, cg_index, cg_table, blocks, *rights[q * ROUN...  9.38 us
    unnamed x27, local copies, waits for them, and re-layouts  5.65 us
    pallas_call x1, Pallas kernels, per_device(): pl.pallas_call(functools.partial(pick_kernel, bits), out_shape=[jax.Shape...  2.38 us
    pallas_call x1, Pallas kernels, per_device(): pl.pallas_call(functools.partial(total_kernel, count), out_shape=jax.Shap...  2.32 us
  transfers between devices with their start and end apart: 10, of which 4 were waited for; matrix products, arithmetic and copies ran while one was open for 3% of the time, Pallas kernels for 17%

profile of v1, /device:TPU:0, one launch (start us, length us, event | category | flops | bytes accessed | tf_op | source)
XLA Modules:
  0.0 56.5 jit_solution(16261377419599039277)
XLA Ops:
  0.0 1.4 %copy.7.pair_slot = s32[2,4,4,3]{3,2,1,0:T(4,128)} copy(s32[2,4,4,3]{2,1,3,0:T(4,128)} %param.6) | data formatting | bytes 768 | tf_op args[1]
  1.4 2.4 %pick.1 = (bf16[2,2,256,128]{3,2,1,0:T(8,128)(2,1)}, bf16[2,2,256,128]{3,2,1,0:T(8,128)(2,1)}, bf16[2,2,256,128]{3,2,1,0:T(8,128)(2,1)}, bf16[2,2,256,128]{3,2,1,0:T(8,128)(2,1)}) custom-call(s32[2,4,4,3]{3,2,1,0:T(4,128)} %copy.7.pair_slot, bf16[4,2,256,256]{3,2,1,0:T(8,128)(2,1)} %bitcast.4), custom_call_target="tpu_custom_call" | custom-call | tf_op jit(solution)/shard_map/pick/pallas_call | solution.py:139
  3.8 4.1 %collective-permute-start = (bf16[2,2,256,128]{3,2,1,0:T(8,128)(2,1)}, bf16[2,2,256,128]{3,2,1,0:T(8,128)(2,1)S(1)}, u32[]{:S(2)}, u32[]{:S(2)}) collective-permute-start(bf16[2,2,256,128]{3,2,1,0:T(8,128)(2,1)} %get-tuple-element.17), channel_id=1, source_target_pairs={{0,8},{4,12},{8,0},{12,4},{1,9},{5,13},{9,1},{13,5},{2,10},{6,14},... | collective-permute-start | bytes 786440 | tf_op jit(solution)/shard_map/ppermute | solution.py:137
  7.9 1.6 %collective-permute-start.1 = (bf16[2,2,256,128]{3,2,1,0:T(8,128)(2,1)}, bf16[2,2,256,128]{3,2,1,0:T(8,128)(2,1)S(1)}, u32[]{:S(2)}, u32[]{:S(2)}) collective-permute-start(bf16[2,2,256,128]{3,2,1,0:T(8,128)(2,1)} %get-tuple-element.18), channel_id=1, source_target_pairs={{0,4},{4,0},{8,12},{12,8},{1,5},{5,1},{9,13},{13,9},{2,6},{6,2},{1... | collective-permute-start | bytes 786440 | tf_op jit(solution)/shard_map/ppermute | solution.py:137
  9.5 0.3 collective-permute-start.5
  9.8 0.1 collective-permute-start.6
  9.9 0.7 %copy.8.channel = s32[2,4,4,3]{3,2,1,0:T(4,128)} copy(s32[2,4,4,3]{2,1,3,0:T(4,128)S(1)} %copy-done.6) | data formatting | bytes 768 | tf_op args[2]
  10.6 0.7 %copy.9.cg_index = s32[2,4,4,3]{3,2,1,0:T(4,128)} copy(s32[2,4,4,3]{2,1,3,0:T(4,128)S(1)} %copy-done.7) | data formatting | bytes 768 | tf_op args[3]
  11.4 10.4 %collective-permute-done.refs_0_ = bf16[2,2,256,128]{3,2,1,0:T(8,128)(2,1)S(1)} collective-permute-done((bf16[2,2,256,128]{3,2,1,0:T(8,128)(2,1)}, bf16[2,2,256,128]{3,2,1,0:T(8,128)(2,1)S(1)}, u32[]{:S(2)}, u32[]{:S(2)}) %collective-permute-start) | collective-permute-done | bytes 262176 | tf_op jit(solution)/shard_map/ppermute | solution.py:137
  21.8 1.1 %collective-permute-done.1.refs_1_ = bf16[2,2,256,128]{3,2,1,0:T(8,128)(2,1)S(1)} collective-permute-done((bf16[2,2,256,128]{3,2,1,0:T(8,128)(2,1)}, bf16[2,2,256,128]{3,2,1,0:T(8,128)(2,1)S(1)}, u32[]{:S(2)}, u32[]{:S(2)}) %collective-permute-start.1) | collective-permute-done | bytes 262176 | tf_op jit(solution)/shard_map/ppermute | solution.py:137
  22.9 0.7 %copy-done.11 = bf16[2,2,256,128]{3,2,1,0:T(8,128)(2,1)} copy-done((bf16[2,2,256,128]{3,2,1,0:T(8,128)(2,1)}, bf16[2,2,256,128]{3,2,1,0:T(8,128)(2,1)S(1)}, u32[]{:S(2)}) %copy-start.11) | copy-done | bytes 262168
  23.6 4.7 %products.2 = (f32[512,128]{1,0:T(8,128)}, s16[528,128]{1,0:T(8,128)(2,1)}, s16[528,128]{1,0:T(8,128)(2,1)}, s16[528,128]{1,0:T(8,128)(2,1)}) custom-call(s32[2,4,4,3]{3,2,1,0:T(4,128)} %copy.7.pair_slot, s32[2,4,4,3]{3,2,1,0:T(4,128)} %copy.8.channel, s32[2,4,4,3]{3,2,1,0:T(4,128)} %copy.9.cg_index, f32[64]{0:T(128)} %cg_table.3, ...), custom_call_target="tpu_custom_call" | custom-call | flops 1073741824 | bytes 1048576 | tf_op jit(solution)/shard_map/products/pallas_call | solution.py:168
  28.3 0.1 collective-permute-start.2
  28.3 3.2 %collective-permute-start.3 = (s16[528,128]{1,0:T(8,128)(2,1)}, s16[528,128]{1,0:T(8,128)(2,1)S(1)}, u32[]{:S(2)}, u32[]{:S(2)}) collective-permute-start(s16[528,128]{1,0:T(8,128)(2,1)} %get-tuple-element.21), channel_id=1, source_target_pairs={{0,8},{4,12},{8,0},{12,4},{1,9},{5,13},{9,1},{13,5},{2,10},{6,14},... | collective-permute-start | bytes 405512 | tf_op jit(solution)/shard_map/ppermute | solution.py:137
  31.5 1.2 %collective-permute-start.4 = (s16[528,128]{1,0:T(8,128)(2,1)}, s16[528,128]{1,0:T(8,128)(2,1)S(1)}, u32[]{:S(2)}, u32[]{:S(2)}) collective-permute-start(s16[528,128]{1,0:T(8,128)(2,1)} %get-tuple-element.22), channel_id=1, source_target_pairs={{0,12},{4,8},{8,4},{12,0},{1,13},{5,9},{9,5},{13,1},{2,14},{6,10},... | collective-permute-start | bytes 405512 | tf_op jit(solution)/shard_map/ppermute | solution.py:137
  32.7 0.0 collective-permute-done.5.refs_0_
  32.7 0.0 collective-permute-done.6.refs_1_
  32.7 0.7 %copy-done.8 = bf16[2,2,256,128]{3,2,1,0:T(8,128)(2,1)} copy-done((bf16[2,2,256,128]{3,2,1,0:T(8,128)(2,1)}, bf16[2,2,256,128]{3,2,1,0:T(8,128)(2,1)S(1)}, u32[]{:S(2)}) %copy-start.8) | copy-done | bytes 262168
  33.4 0.7 %copy-done.9 = bf16[2,2,256,128]{3,2,1,0:T(8,128)(2,1)} copy-done((bf16[2,2,256,128]{3,2,1,0:T(8,128)(2,1)}, bf16[2,2,256,128]{3,2,1,0:T(8,128)(2,1)S(1)}, u32[]{:S(2)}) %copy-start.9) | copy-done | bytes 262168
  34.1 4.7 %products.3 = (f32[512,128]{1,0:T(8,128)}, s16[528,128]{1,0:T(8,128)(2,1)}, s16[528,128]{1,0:T(8,128)(2,1)}, s16[528,128]{1,0:T(8,128)(2,1)}) custom-call(s32[2,4,4,3]{3,2,1,0:T(4,128)} %copy.7.pair_slot, s32[2,4,4,3]{3,2,1,0:T(4,128)} %copy.8.channel, s32[2,4,4,3]{3,2,1,0:T(4,128)} %copy.9.cg_index, f32[64]{0:T(128)} %cg_table.3, ...), custom_call_target="tpu_custom_call" | custom-call | flops 1073741824 | bytes 1048576 | tf_op jit(solution)/shard_map/products/pallas_call | solution.py:168
  38.8 0.8 %collective-permute-start.7 = (s16[528,128]{1,0:T(8,128)(2,1)}, s16[528,128]{1,0:T(8,128)(2,1)S(1)}, u32[]{:S(2)}, u32[]{:S(2)}) collective-permute-start(s16[528,128]{1,0:T(8,128)(2,1)} %get-tuple-element.26), channel_id=1, source_target_pairs={{0,4},{4,0},{8,12},{12,8},{1,5},{5,1},{9,13},{13,9},{2,6},{6,2},{1... | collective-permute-start | bytes 405512 | tf_op jit(solution)/shard_map/ppermute | solution.py:137
  39.6 2.4 %collective-permute-start.8 = (s16[528,128]{1,0:T(8,128)(2,1)}, s16[528,128]{1,0:T(8,128)(2,1)S(1)}, u32[]{:S(2)}, u32[]{:S(2)}) collective-permute-start(s16[528,128]{1,0:T(8,128)(2,1)} %get-tuple-element.27), channel_id=1, source_target_pairs={{0,8},{4,12},{8,0},{12,4},{1,9},{5,13},{9,1},{13,5},{2,10},{6,14},... | collective-permute-start | bytes 405512 | tf_op jit(solution)/shard_map/ppermute | solution.py:137
  42.0 0.0 collective-permute-done.2.refs_1_
  42.0 1.2 %collective-permute-start.9 = (s16[528,128]{1,0:T(8,128)(2,1)}, s16[528,128]{1,0:T(8,128)(2,1)S(1)}, u32[]{:S(2)}, u32[]{:S(2)}) collective-permute-start(s16[528,128]{1,0:T(8,128)(2,1)} %get-tuple-element.28), channel_id=1, source_target_pairs={{0,12},{4,8},{8,4},{12,0},{1,13},{5,9},{9,5},{13,1},{2,14},{6,10},... | collective-permute-start | bytes 405512 | tf_op jit(solution)/shard_map/ppermute | solution.py:137
  43.2 0.0 collective-permute-done.3.refs_2_
  43.2 0.0 collective-permute-done.4.refs_3_
  43.2 2.3 %collective-permute-done.7.refs_5_ = s16[528,128]{1,0:T(8,128)(2,1)S(1)} collective-permute-done((s16[528,128]{1,0:T(8,128)(2,1)}, s16[528,128]{1,0:T(8,128)(2,1)S(1)}, u32[]{:S(2)}, u32[]{:S(2)}) %collective-permute-start.7) | collective-permute-done | bytes 135200 | tf_op jit(solution)/shard_map/ppermute | solution.py:137
  45.5 8.1 %collective-permute-done.8.refs_6_ = s16[528,128]{1,0:T(8,128)(2,1)S(1)} collective-permute-done((s16[528,128]{1,0:T(8,128)(2,1)}, s16[528,128]{1,0:T(8,128)(2,1)S(1)}, u32[]{:S(2)}, u32[]{:S(2)}) %collective-permute-start.8) | collective-permute-done | bytes 135200 | tf_op jit(solution)/shard_map/ppermute | solution.py:137
  53.5 0.0 collective-permute-done.9.refs_7_
  53.6 0.6 %copy-done.4 = s16[528,128]{1,0:T(8,128)(2,1)} copy-done((s16[528,128]{1,0:T(8,128)(2,1)}, s16[528,128]{1,0:T(8,128)(2,1)S(1)}, u32[]{:S(2)}) %copy-start.4) | copy-done | bytes 135192
  54.2 0.1 copy-done.5
  54.2 2.3 %total.1 = bf16[4,2,64,256]{3,2,1,0:T(8,128)(2,1)} custom-call(f32[512,128]{1,0:T(8,128)} %get-tuple-element.19.refs_0_, s16[528,128]{1,0:T(8,128)(2,1)} %copy-done, s16[528,128]{1,0:T(8,128)(2,1)} %copy-done.1, s16[528,128]{1,0:T(8,128)(2,1)} %copy-done.2, f32[512,128]{1,0:T(8,128)} %get-tuple-element.25.refs_4_, s16[528,128]{1,0:T(8,128)(2,1)} %copy-done.3, ...), custom_call_target="tpu_custom_call" | custom-call | tf_op jit(solution)/shard_map/total/pallas_call | solution.py:173
  (19 shorter events, 0.0 us)
Async XLA Ops:
  1.4 8.5 %copy-start.6 = (s32[2,4,4,3]{2,1,3,0:T(4,128)S(1)}, s32[2,4,4,3]{2,1,3,0:T(4,128)}, u32[]{:S(2)}) copy-start(s32[2,4,4,3]{2,1,3,0:T(4,128)} %param.7) | copy-start | bytes 1156
  3.8 18.0 %collective-permute-start = (bf16[2,2,256,128]{3,2,1,0:T(8,128)(2,1)}, bf16[2,2,256,128]{3,2,1,0:T(8,128)(2,1)S(1)}, u32[]{:S(2)}, u32[]{:S(2)}) collective-permute-start(bf16[2,2,256,128]{3,2,1,0:T(8,128)(2,1)} %get-tuple-element.17), channel_id=1, source_target_pairs={{0,8},{4,12},{8,0},{12,4},{1,9},{5,13},{9,1},{13,5},{2,10},{6,14},... | collective-permute-start | bytes 786440 | tf_op jit(solution)/shard_map/ppermute | solution.py:137
  7.9 15.0 %collective-permute-start.1 = (bf16[2,2,256,128]{3,2,1,0:T(8,128)(2,1)}, bf16[2,2,256,128]{3,2,1,0:T(8,128)(2,1)S(1)}, u32[]{:S(2)}, u32[]{:S(2)}) collective-permute-start(bf16[2,2,256,128]{3,2,1,0:T(8,128)(2,1)} %get-tuple-element.18), channel_id=1, source_target_pairs={{0,4},{4,0},{8,12},{12,8},{1,5},{5,1},{9,13},{13,9},{2,6},{6,2},{1... | collective-permute-start | bytes 786440 | tf_op jit(solution)/shard_map/ppermute | solution.py:137
  9.5 23.2 %collective-permute-start.5 = (bf16[2,2,256,128]{3,2,1,0:T(8,128)(2,1)}, bf16[2,2,256,128]{3,2,1,0:T(8,128)(2,1)S(1)}, u32[]{:S(2)}, u32[]{:S(2)}) collective-permute-start(bf16[2,2,256,128]{3,2,1,0:T(8,128)(2,1)} %get-tuple-element.23), channel_id=1, source_target_pairs={{0,8},{4,12},{8,0},{12,4},{1,9},{5,13},{9,1},{13,5},{2,10},{6,14},... | collective-permute-start | bytes 786440 | tf_op jit(solution)/shard_map/ppermute | solution.py:137
  9.8 0.8 %copy-start.7 = (s32[2,4,4,3]{2,1,3,0:T(4,128)S(1)}, s32[2,4,4,3]{2,1,3,0:T(4,128)}, u32[]{:S(2)}) copy-start(s32[2,4,4,3]{2,1,3,0:T(4,128)} %param.8) | copy-start | bytes 1156
  9.8 22.9 %collective-permute-start.6 = (bf16[2,2,256,128]{3,2,1,0:T(8,128)(2,1)}, bf16[2,2,256,128]{3,2,1,0:T(8,128)(2,1)S(1)}, u32[]{:S(2)}, u32[]{:S(2)}) collective-permute-start(bf16[2,2,256,128]{3,2,1,0:T(8,128)(2,1)} %get-tuple-element.24), channel_id=1, source_target_pairs={{0,4},{4,0},{8,12},{12,8},{1,5},{5,1},{9,13},{13,9},{2,6},{6,2},{1... | collective-permute-start | bytes 786440 | tf_op jit(solution)/shard_map/ppermute | solution.py:137
  21.8 1.1 %copy-start.10 = (bf16[2,2,256,128]{3,2,1,0:T(8,128)(2,1)}, bf16[2,2,256,128]{3,2,1,0:T(8,128)(2,1)S(1)}, u32[]{:S(2)}) copy-start(bf16[2,2,256,128]{3,2,1,0:T(8,128)(2,1)S(1)} %collective-permute-done.refs_0_) | copy-start | bytes 786436
  22.9 0.7 %copy-start.11 = (bf16[2,2,256,128]{3,2,1,0:T(8,128)(2,1)}, bf16[2,2,256,128]{3,2,1,0:T(8,128)(2,1)S(1)}, u32[]{:S(2)}) copy-start(bf16[2,2,256,128]{3,2,1,0:T(8,128)(2,1)S(1)} %collective-permute-done.1.refs_1_) | copy-start | bytes 786436
  28.3 13.7 %collective-permute-start.2 = (s16[528,128]{1,0:T(8,128)(2,1)}, s16[528,128]{1,0:T(8,128)(2,1)S(1)}, u32[]{:S(2)}, u32[]{:S(2)}) collective-permute-start(s16[528,128]{1,0:T(8,128)(2,1)} %get-tuple-element.20), channel_id=1, source_target_pairs={{0,4},{4,0},{8,12},{12,8},{1,5},{5,1},{9,13},{13,9},{2,6},{6,2},{1... | collective-permute-start | bytes 405512 | tf_op jit(solution)/shard_map/ppermute | solution.py:137
  28.3 14.8 %collective-permute-start.3 = (s16[528,128]{1,0:T(8,128)(2,1)}, s16[528,128]{1,0:T(8,128)(2,1)S(1)}, u32[]{:S(2)}, u32[]{:S(2)}) collective-permute-start(s16[528,128]{1,0:T(8,128)(2,1)} %get-tuple-element.21), channel_id=1, source_target_pairs={{0,8},{4,12},{8,0},{12,4},{1,9},{5,13},{9,1},{13,5},{2,10},{6,14},... | collective-permute-start | bytes 405512 | tf_op jit(solution)/shard_map/ppermute | solution.py:137
  31.5 11.7 %collective-permute-start.4 = (s16[528,128]{1,0:T(8,128)(2,1)}, s16[528,128]{1,0:T(8,128)(2,1)S(1)}, u32[]{:S(2)}, u32[]{:S(2)}) collective-permute-start(s16[528,128]{1,0:T(8,128)(2,1)} %get-tuple-element.22), channel_id=1, source_target_pairs={{0,12},{4,8},{8,4},{12,0},{1,13},{5,9},{9,5},{13,1},{2,14},{6,10},... | collective-permute-start | bytes 405512 | tf_op jit(solution)/shard_map/ppermute | solution.py:137
  32.7 0.7 %copy-start.8 = (bf16[2,2,256,128]{3,2,1,0:T(8,128)(2,1)}, bf16[2,2,256,128]{3,2,1,0:T(8,128)(2,1)S(1)}, u32[]{:S(2)}) copy-start(bf16[2,2,256,128]{3,2,1,0:T(8,128)(2,1)S(1)} %collective-permute-done.5.refs_0_) | copy-start | bytes 786436
  33.4 0.7 %copy-start.9 = (bf16[2,2,256,128]{3,2,1,0:T(8,128)(2,1)}, bf16[2,2,256,128]{3,2,1,0:T(8,128)(2,1)S(1)}, u32[]{:S(2)}) copy-start(bf16[2,2,256,128]{3,2,1,0:T(8,128)(2,1)S(1)} %collective-permute-done.6.refs_1_) | copy-start | bytes 786436
  38.8 6.7 %collective-permute-start.7 = (s16[528,128]{1,0:T(8,128)(2,1)}, s16[528,128]{1,0:T(8,128)(2,1)S(1)}, u32[]{:S(2)}, u32[]{:S(2)}) collective-permute-start(s16[528,128]{1,0:T(8,128)(2,1)} %get-tuple-element.26), channel_id=1, source_target_pairs={{0,4},{4,0},{8,12},{12,8},{1,5},{5,1},{9,13},{13,9},{2,6},{6,2},{1... | collective-permute-start | bytes 405512 | tf_op jit(solution)/shard_map/ppermute | solution.py:137
  39.6 13.9 %collective-permute-start.8 = (s16[528,128]{1,0:T(8,128)(2,1)}, s16[528,128]{1,0:T(8,128)(2,1)S(1)}, u32[]{:S(2)}, u32[]{:S(2)}) collective-permute-start(s16[528,128]{1,0:T(8,128)(2,1)} %get-tuple-element.27), channel_id=1, source_target_pairs={{0,8},{4,12},{8,0},{12,4},{1,9},{5,13},{9,1},{13,5},{2,10},{6,14},... | collective-permute-start | bytes 405512 | tf_op jit(solution)/shard_map/ppermute | solution.py:137
  42.0 11.5 %copy-start = (s16[528,128]{1,0:T(8,128)(2,1)}, s16[528,128]{1,0:T(8,128)(2,1)S(1)}, u32[]{:S(2)}) copy-start(s16[528,128]{1,0:T(8,128)(2,1)S(1)} %collective-permute-done.2.refs_1_) | copy-start | bytes 405508
  42.0 11.5 %collective-permute-start.9 = (s16[528,128]{1,0:T(8,128)(2,1)}, s16[528,128]{1,0:T(8,128)(2,1)S(1)}, u32[]{:S(2)}, u32[]{:S(2)}) collective-permute-start(s16[528,128]{1,0:T(8,128)(2,1)} %get-tuple-element.28), channel_id=1, source_target_pairs={{0,12},{4,8},{8,4},{12,0},{1,13},{5,9},{9,5},{13,1},{2,14},{6,10},... | collective-permute-start | bytes 405512 | tf_op jit(solution)/shard_map/ppermute | solution.py:137
  43.2 10.4 %copy-start.1 = (s16[528,128]{1,0:T(8,128)(2,1)}, s16[528,128]{1,0:T(8,128)(2,1)S(1)}, u32[]{:S(2)}) copy-start(s16[528,128]{1,0:T(8,128)(2,1)S(1)} %collective-permute-done.3.refs_2_) | copy-start | bytes 405508
  43.2 10.4 %copy-start.2 = (s16[528,128]{1,0:T(8,128)(2,1)}, s16[528,128]{1,0:T(8,128)(2,1)S(1)}, u32[]{:S(2)}) copy-start(s16[528,128]{1,0:T(8,128)(2,1)S(1)} %collective-permute-done.4.refs_3_) | copy-start | bytes 405508
  45.5 8.1 %copy-start.3 = (s16[528,128]{1,0:T(8,128)(2,1)}, s16[528,128]{1,0:T(8,128)(2,1)S(1)}, u32[]{:S(2)}) copy-start(s16[528,128]{1,0:T(8,128)(2,1)S(1)} %collective-permute-done.7.refs_5_) | copy-start | bytes 405508
  53.5 0.7 %copy-start.4 = (s16[528,128]{1,0:T(8,128)(2,1)}, s16[528,128]{1,0:T(8,128)(2,1)S(1)}, u32[]{:S(2)}) copy-start(s16[528,128]{1,0:T(8,128)(2,1)S(1)} %collective-permute-done.8.refs_6_) | copy-start | bytes 405508
  53.5 0.7 %copy-start.5 = (s16[528,128]{1,0:T(8,128)(2,1)}, s16[528,128]{1,0:T(8,128)(2,1)S(1)}, u32[]{:S(2)}) copy-start(s16[528,128]{1,0:T(8,128)(2,1)S(1)} %collective-permute-done.9.refs_7_) | copy-start | bytes 405508
